TPU v7x, 32 devices: a whole 2x2x4 slice. The times are simulated.
32 devices in a mesh: dp: 4 (over z), seqhi: 2 (over x), seqlo: 4 (over y, core).
Axes of the slice: x: 2, y: 2, z: 4, core: 2. Of those that a mesh axis runs over, the one named last changes fastest.
Arguments:
- queries: bfloat16 [4, 2048, 384], P('dp', ('seqhi', 'seqlo')), may hold values from -2 to 2
- key_rows: bfloat16 [4, 2048, 384], P('dp', ('seqhi', 'seqlo')), may hold values from -2 to 2
- value_rows: bfloat16 [4, 2048, 384], P('dp', ('seqhi', 'seqlo')), may hold values from -3 to 3
- head_scale: float32 [6], replicated, may hold values from 0.15 to 1
- out_weight: bfloat16 [384, 384], replicated, may hold values from -0.3125 to 0.3125
- cotangent: bfloat16 [4, 2048, 384], P('dp', ('seqhi', 'seqlo')), may hold values from -6 to 6
Outputs:
- queries_gradient: bfloat16 [4, 2048, 384], P('dp', ('seqhi', 'seqlo'))
- keys_gradient: bfloat16 [4, 2048, 384], P('dp', ('seqhi', 'seqlo'))
- values_gradient: bfloat16 [4, 2048, 384], P('dp', ('seqhi', 'seqlo'))
- weight_gradient: float32 [384, 384], P('dp')
All inputs are finite; a program needn't handle non-finite values.
Results may differ from a plain program's by a relative error of at most 0.025.
Values may be sent and summed in bfloat16 or wider, within the bound.
No kernel may reach another device: no remote copies, remote signals or barrier semaphores. Data moves between devices by JAX's collectives and lax.ppermute only.
A program may use at most 64 MiB of HBM per device.

v0:
```python
import jax
import jax.numpy as jnp
from jax import lax
from jax.sharding import PartitionSpec as P


def swapped(value, axis, stride):
    mask = 2**stride
    pairs = [(source, source ^ mask) for source in range(lax.axis_size(axis))]
    return lax.ppermute(value, axis, pairs)


def split_heads(matrix, head_count):
    return matrix.reshape(matrix.shape[0], head_count, matrix.shape[1] // head_count)


def pair_mean(matrix):
    paired = matrix.astype(jnp.float32).reshape(matrix.shape[0] // 2, 2, matrix.shape[1])
    return (0.5 * (paired[:, 0] + paired[:, 1])).astype(jnp.bfloat16)


def pair_total(matrix):
    paired = matrix.astype(jnp.float32).reshape(matrix.shape[0] // 2, 2, matrix.shape[1])
    return (paired[:, 0] + paired[:, 1]).astype(jnp.bfloat16)


def spread_rows(matrix, factor):
    widened = jnp.broadcast_to(matrix[:, None], (matrix.shape[0], factor) + matrix.shape[1:])
    return widened.reshape((matrix.shape[0] * factor,) + matrix.shape[1:])


def group_sum(matrix, factor):
    return jnp.sum(matrix.reshape((matrix.shape[0] // factor, factor) + matrix.shape[1:]), axis=1)


def score_terms(queries, key_block, scales):
    head_count = scales.shape[0]
    factor = scales / jnp.sqrt(jnp.float32(queries.shape[1] // head_count))
    logits = jnp.einsum(
        "rhe,che->hrc",
        split_heads(queries, head_count),
        split_heads(key_block, head_count),
        preferred_element_type=jnp.float32,
    )
    return (jnp.exp(logits * factor[:, None, None]), factor)


def attend(queries, key_block, value_block, scales, multiplicity):
    head_count = scales.shape[0]
    weights, factor = score_terms(queries, key_block, scales)
    probabilities = weights.astype(jnp.bfloat16)
    numerator = jnp.einsum(
        "hrc,che->rhe",
        probabilities,
        split_heads(value_block, head_count),
        preferred_element_type=jnp.float32,
    )
    numerator = numerator.reshape(queries.shape[0], queries.shape[1])
    denominator = multiplicity * jnp.sum(weights, axis=2).T
    return (numerator, denominator)


def attend_back(queries, key_block, value_block, scales, multiplicity, numer_grad, denom_grad):
    head_count = scales.shape[0]
    weights, factor = score_terms(queries, key_block, scales)
    probabilities = weights.astype(jnp.bfloat16)
    grad_heads = split_heads(numer_grad, head_count)
    prob_grad = jnp.einsum(
        "rhe,che->hrc",
        grad_heads,
        split_heads(value_block, head_count),
        preferred_element_type=jnp.float32,
    )
    logit_grad = (
        weights * (prob_grad + multiplicity * denom_grad.T[:, :, None]) * factor[:, None, None]
    ).astype(jnp.bfloat16)
    query_piece = jnp.einsum(
        "hrc,che->rhe",
        logit_grad,
        split_heads(key_block, head_count),
        preferred_element_type=jnp.float32,
    ).reshape(queries.shape)
    key_piece = jnp.einsum(
        "hrc,rhe->che",
        logit_grad,
        split_heads(queries, head_count),
        preferred_element_type=jnp.float32,
    ).reshape(key_block.shape)
    value_piece = jnp.einsum(
        "hrc,rhe->che", probabilities, grad_heads, preferred_element_type=jnp.float32
    ).reshape(value_block.shape)
    return (query_piece, key_piece, value_piece)


def shards(queries, key_rows, value_rows, head_scale, out_weight, cotangent):
    query_local = queries[0]
    key_local = key_rows[0]
    value_local = value_rows[0]
    cotan_local = cotangent[0]
    head_count = head_scale.shape[0]
    feature_width = query_local.shape[1]
    block_rows = key_local.shape[0] // 2
    top_level = lax.axis_size(("seqhi", "seqlo")).bit_length() - 1
    position = lax.axis_index(("seqhi", "seqlo"))
    numerator, denominator = attend(query_local, key_local, value_local, head_scale, 1.0)
    coarse_queries = [query_local]
    sibling_pairs = [None]
    level_numers = [None]
    level_denoms = [None]
    own_keys = pair_mean(key_local)
    own_values = pair_total(value_local)
    for height in range(1, top_level + 1):
        coarse_queries.append(pair_mean(coarse_queries[-1]))
        if height > 1:
            lower_first = position // 2 ** (height - 2) % 2 == 0
            sib_keys, sib_values = sibling_pairs[-1]
            own_keys = pair_mean(
                jnp.concatenate(
                    [
                        jnp.where(lower_first, own_keys, sib_keys),
                        jnp.where(lower_first, sib_keys, own_keys),
                    ],
                    axis=0,
                )
            )
            own_values = pair_total(
                jnp.concatenate(
                    [
                        jnp.where(lower_first, own_values, sib_values),
                        jnp.where(lower_first, sib_values, own_values),
                    ],
                    axis=0,
                )
            )
        arrived = swapped((own_keys, own_values), ("seqhi", "seqlo"), height - 1)
        sibling_pairs.append(arrived)
        level_numer, level_denom = attend(
            coarse_queries[height], arrived[0], arrived[1], head_scale, float(2**height)
        )
        level_numers.append(level_numer)
        level_denoms.append(level_denom)
    numer_acc = level_numers[top_level]
    denom_acc = level_denoms[top_level]
    for height in range(top_level - 1, 0, -1):
        numer_acc = level_numers[height] + spread_rows(numer_acc, 2)
        denom_acc = level_denoms[height] + spread_rows(denom_acc, 2)
    numerator = numerator + spread_rows(numer_acc, 2)
    denominator = denominator + spread_rows(denom_acc, 2)
    attended_heads = split_heads(numerator, head_count) / denominator[:, :, None]
    attended = attended_heads.reshape(numerator.shape).astype(jnp.bfloat16)
    own_rows = feature_width // lax.axis_size("dp")
    weight_term = lax.dot_general(
        attended, cotan_local, (((0,), (0,)), ((), ())), preferred_element_type=jnp.float32
    )
    summed = lax.psum(weight_term, ("dp", "seqhi", "seqlo"))
    weight_gradient = lax.dynamic_slice_in_dim(summed, lax.axis_index("dp") * own_rows, own_rows, 0)
    backward = lax.dot_general(
        cotan_local, out_weight, (((1,), (1,)), ((), ())), preferred_element_type=jnp.float32
    ).astype(jnp.bfloat16)
    back_heads = split_heads(backward, head_count).astype(jnp.float32)
    numer_grad = (back_heads / denominator[:, :, None]).reshape(numerator.shape)
    denom_grad = -jnp.sum(back_heads * attended_heads, axis=2) / denominator
    query_grad, key_grad, value_grad = attend_back(
        query_local,
        key_local,
        value_local,
        head_scale,
        1.0,
        numer_grad.astype(jnp.bfloat16),
        denom_grad,
    )
    level_query_grads = [None]
    level_key_sends = [None]
    numer_group = numer_grad
    denom_group = denom_grad
    for height in range(1, top_level + 1):
        numer_group = group_sum(numer_group, 2)
        denom_group = group_sum(denom_group, 2)
        query_piece, key_piece, value_piece = attend_back(
            coarse_queries[height],
            sibling_pairs[height][0],
            sibling_pairs[height][1],
            head_scale,
            float(2**height),
            numer_group.astype(jnp.bfloat16),
            denom_group,
        )
        level_query_grads.append(query_piece)
        level_key_sends.append((key_piece, value_piece))
    chain_query = level_query_grads[top_level]
    for height in range(top_level - 1, 0, -1):
        chain_query = level_query_grads[height] + spread_rows(0.5 * chain_query, 2)
    query_total = query_grad + spread_rows(0.5 * chain_query, 2)
    returned = [None]
    for height in range(1, top_level + 1):
        returned.append(swapped(level_key_sends[height], ("seqhi", "seqlo"), height - 1))
    carry_pair = returned[top_level]
    for height in range(top_level - 1, 0, -1):
        up_keys = spread_rows(0.5 * carry_pair[0], 2)
        up_values = spread_rows(carry_pair[1], 2)
        split_lower_first = position // 2 ** (height - 1) % 2 == 0
        own_pair = (
            jnp.where(split_lower_first, up_keys[:block_rows], up_keys[block_rows:]),
            jnp.where(split_lower_first, up_values[:block_rows], up_values[block_rows:]),
        )
        other_pair = (
            jnp.where(split_lower_first, up_keys[block_rows:], up_keys[:block_rows]),
            jnp.where(split_lower_first, up_values[block_rows:], up_values[:block_rows]),
        )
        own_pair, other_pair = (own_pair, other_pair)
        parent = swapped((other_pair[0], other_pair[1]), ("seqhi", "seqlo"), height - 1)
        carry_pair = (
            own_pair[0] + parent[0] + returned[height][0],
            own_pair[1] + parent[1] + returned[height][1],
        )
    key_total = key_grad + spread_rows(0.5 * carry_pair[0], 2)
    value_total = value_grad + spread_rows(carry_pair[1], 2)
    return (
        query_total.astype(jnp.bfloat16)[None],
        key_total.astype(jnp.bfloat16)[None],
        value_total.astype(jnp.bfloat16)[None],
        weight_gradient,
    )


def solution(mesh):
    in_specs = (
        P("dp", ("seqhi", "seqlo"), None),
        P("dp", ("seqhi", "seqlo"), None),
        P("dp", ("seqhi", "seqlo"), None),
        P(),
        P(),
        P("dp", ("seqhi", "seqlo"), None),
    )
    out_specs = (
        P("dp", ("seqhi", "seqlo"), None),
        P("dp", ("seqhi", "seqlo"), None),
        P("dp", ("seqhi", "seqlo"), None),
        P("dp", None),
    )
    return jax.shard_map(shards, mesh=mesh, in_specs=in_specs, out_specs=out_specs, check_vma=False)
```

profile of v0, /device:TPU:1, one launch (start us, length us, event | category | flops | bytes accessed | tf_op | source)
XLA Modules:
  0.0 210.4 jit_solution(2963989376022502578)
XLA Ops:
  7.2 1.2 reshape.433
  8.5 0.3 fusion.63
  9.1 0.3 fusion.59
  9.5 0.5 collective-permute-start.3
  10.2 0.8 copy.316
  11.4 0.3 fusion.60
  12.0 0.4 convert_reduce_fusion.1
  12.9 0.4 fusion.67
  13.5 0.7 convert_element_type.251
  14.5 0.3 fusion.58
  14.9 0.7 fusion.37
  15.5 2.3 %collective-permute-start.4 = (bf16[128,384]{1,0:T(8,128)(2,1)}, bf16[128,384]{1,0:T(8,128)(2,1)S(1)}, u32[]{:S(2)}, u32[]{:S(2)}) collective-permute-start(bf16[128,384]{1,0:T(8,128)(2,1)} %fusion.37), channel_id=1, source_target_pairs={{0,2},{1,3},{2,0},{3,1},{4,6},{5,7},{6,4},{7,5},{8,10},{9,11},{10,... | collective-permute-start | bytes 294920 | tf_op jit(solution)/shard_map/ppermute | solution.py:10
  18.4 0.7 fusion.34
  20.0 0.8 collective-permute-done.4
  20.8 1.0 broadcast_select_fusion.1
  22.3 0.6 copy.454
  22.9 1.1 collective-permute-start.5
  24.0 1.0 broadcast_select_fusion.3
  25.6 0.4 collective-permute-start.2
  26.1 1.0 copy.302
  27.1 0.3 fusion.65
  27.4 1.0 copy.325
  28.6 0.8 copy.328
  30.7 1.9 divide_convert_fusion
  32.6 0.8 copy.388
  33.4 0.9 copy.317
  34.3 1.0 reshape.442
  35.3 1.0 copy.326
  37.1 0.9 broadcast_in_dim.46
  38.0 1.5 reshape.410
  39.5 1.0 copy.330
  40.5 1.1 copy.315
  41.7 1.1 fusion.16
  42.8 1.0 fusion.57
  43.7 0.8 copy.335
  44.6 0.4 multiply_convert_fusion
  45.0 0.4 fusion.70
  45.9 0.3 div.50.clone
  46.2 1.4 div.55
  47.6 1.6 divide_reduce_fusion
  49.7 0.6 convert_element_type.281
  52.8 0.9 fusion.68
  53.8 0.9 copy.390
  54.7 0.8 fusion.44
  56.7 2.1 %fusion.30 = f32[384,384]{1,0:T(8,128)} fusion(bf16[256,384]{0,1:T(8,128)(2,1)} %bitcast.190, bf16[1,256,384]{2,1,0:T(8,128)(2,1)} %param.11), kind=kOutput, calls=%fused_computation.59 | convolution fusion | flops 75497472 | bytes 983040 | tf_op jit(solution)/shard_map/dot_general | solution.py:152
  59.0 0.8 copy.357
  60.1 0.8 copy.349
  62.3 2.4 %collective-permute-start.8 = (f32[128,384]{1,0:T(8,128)S(1)}, f32[128,384]{1,0:T(8,128)}, u32[]{:S(2)}, u32[]{:S(2)}) collective-permute-start(f32[128,384]{1,0:T(8,128)S(1)} %copy.351), channel_id=1, source_target_pairs={{0,2},{1,3},{2,0},{3,1},{4,6},{5,7},{6,4},{7,5},{8,10},{9,11},{10,... | collective-permute-start | bytes 589832 | tf_op jit(solution)/shard_map/ppermute | solution.py:10
  64.7 2.4 %collective-permute-start.10 = (f32[128,384]{1,0:T(8,128)S(1)}, f32[128,384]{1,0:T(8,128)}, u32[]{:S(2)}, u32[]{:S(2)}) collective-permute-start(f32[128,384]{1,0:T(8,128)S(1)} %copy.353), channel_id=1, source_target_pairs={{0,1},{1,0},{2,3},{3,2},{4,5},{5,4},{6,7},{7,6},{8,9},{9,8},{10,11... | collective-permute-start | bytes 589832 | tf_op jit(solution)/shard_map/ppermute | solution.py:10
  67.0 0.5 collective-permute-start.6
  67.5 0.7 add_convert_fusion.2
  68.2 5.9 %collective-permute-done.6 = f32[128,384]{1,0:T(8,128)S(1)} collective-permute-done((f32[128,384]{1,0:T(8,128)}, f32[128,384]{1,0:T(8,128)S(1)}, u32[]{:S(2)}, u32[]{:S(2)}) %collective-permute-start.6) | collective-permute-done | bytes 196640 | tf_op jit(solution)/shard_map/ppermute | solution.py:10
  74.4 5.4 %collective-permute-done.11 = f32[128,384]{1,0:T(8,128)S(1)} collective-permute-done((f32[128,384]{1,0:T(8,128)S(1)}, f32[128,384]{1,0:T(8,128)S(1)}, u32[]{:S(2)}, u32[]{:S(2)}) %collective-permute-start.11) | collective-permute-done | bytes 196640 | tf_op jit(solution)/shard_map/ppermute | solution.py:10
  80.5 109.2 %all-reduce.2.cloned.1.call-done = f32[384,384]{1,0:T(8,128)} async-done(((f32[384,384]{1,0:T(8,128)}), f32[384,384]{1,0:T(8,128)}) %all-reduce.2.cloned.1.call-update) | async-done | bytes 589840 | tf_op jit(solution)/shard_map/psum | solution.py:155
  189.7 1.6 constant_dynamic-slice_fusion
  191.3 1.1 collective-permute-start.12
  192.4 1.0 add_multiply_fusion.1
  193.8 0.6 collective-permute-start.9
  194.4 3.2 %collective-permute-done.12 = f32[128,384]{1,0:T(8,128)} collective-permute-done((f32[128,384]{1,0:T(8,128)S(1)}, f32[128,384]{1,0:T(8,128)}, u32[]{:S(2)}, u32[]{:S(2)}) %collective-permute-start.12) | collective-permute-done | bytes 196640 | tf_op jit(solution)/shard_map/ppermute | solution.py:10
  197.6 1.1 add_add_fusion.1
  199.2 1.1 collective-permute-start.14
  200.3 1.0 add_multiply_fusion
  202.2 0.7 add_convert_fusion.1
  202.9 0.7 add_convert_fusion
  (238 shorter events, 15.4 us)
Async XLA Ops:
  7.2 23.5 %copy-start = (bf16[384,384]{1,0:T(8,128)(2,1)S(1)}, bf16[384,384]{1,0:T(8,128)(2,1)}, u32[]{:S(2)}) copy-start(bf16[384,384]{1,0:T(8,128)(2,1)} %param.10) | copy-start | bytes 884740
  7.2 1.8 copy-start.29
  7.2 182.5 %all-reduce.2.cloned.1.call-start = ((), (), s32[]{:S(2)}) async-start(), calls=%async_computation | async-start | bytes 1179648 | tf_op jit(solution)/shard_map/psum | solution.py:155
  8.4 1.6 copy-start.28
  8.8 2.2 %copy-start.30 = (bf16[1,256,384]{2,1,0:T(8,128)(2,1)S(1)}, bf16[1,256,384]{2,1,0:T(8,128)(2,1)}, u32[]{:S(2)}) copy-start(bf16[1,256,384]{2,1,0:T(8,128)(2,1)} %param.6) | copy-start | bytes 589828
  8.8 5.4 %collective-permute-start = (bf16[128,384]{1,0:T(8,128)(2,1)S(1)}, bf16[128,384]{1,0:T(8,128)(2,1)S(1)}, u32[]{:S(2)}, u32[]{:S(2)}) collective-permute-start(bf16[128,384]{1,0:T(8,128)(2,1)S(1)} %fusion.33), channel_id=1, source_target_pairs={{0,1},{1,0},{2,3},{3,2},{4,5},{5,4},{6,7},{7,6},{8,9},{9,8},{10,11... | collective-permute-start | bytes 294920 | tf_op jit(solution)/shard_map/ppermute | solution.py:10
  9.5 4.7 %collective-permute-start.3 = (bf16[128,384]{1,0:T(8,128)(2,1)S(1)}, bf16[128,384]{1,0:T(8,128)(2,1)S(1)}, u32[]{:S(2)}, u32[]{:S(2)}) collective-permute-start(bf16[128,384]{1,0:T(8,128)(2,1)S(1)} %fusion.36), channel_id=1, source_target_pairs={{0,1},{1,0},{2,3},{3,2},{4,5},{5,4},{6,7},{7,6},{8,9},{9,8},{10,11... | collective-permute-start | bytes 294920 | tf_op jit(solution)/shard_map/ppermute | solution.py:10
  10.2 2.7 %copy-start.1 = (bf16[1,256,384]{1,2,0:T(8,128)(2,1)}, bf16[1,256,384]{1,2,0:T(8,128)(2,1)S(1)}, u32[]{:S(2)}) copy-start(bf16[1,256,384]{1,2,0:T(8,128)(2,1)S(1)} %copy.293) | copy-start | bytes 589828
  10.2 1.8 copy-start.42
  11.2 1.7 copy-start.3
  11.8 7.4 %copy-start.22 = (bf16[128,1,384]{0,2,1:T(8,128)(2,1)}, bf16[128,1,384]{0,2,1:T(8,128)(2,1)S(1)}, u32[]{:S(2)}) copy-start(bf16[128,1,384]{0,2,1:T(8,128)(2,1)S(1)} %copy.296) | copy-start | bytes 294916
  12.0 17.5 %copy-start.40 = (f32[6]{0:T(128)}, f32[6]{0:T(128)S(1)}, u32[]{:S(2)}) copy-start(f32[6]{0:T(128)S(1)} %broadcast_multiply_fusion.1) | copy-start | bytes 76
  12.5 14.6 %copy-start.12 = (bf16[64,384]{0,1:T(8,128)(2,1)}, bf16[64,384]{0,1:T(8,128)(2,1)S(1)}, u32[]{:S(2)}) copy-start(bf16[64,384]{0,1:T(8,128)(2,1)S(1)} %copy.389) | copy-start | bytes 147460
  15.5 5.3 %collective-permute-start.4 = (bf16[128,384]{1,0:T(8,128)(2,1)}, bf16[128,384]{1,0:T(8,128)(2,1)S(1)}, u32[]{:S(2)}, u32[]{:S(2)}) collective-permute-start(bf16[128,384]{1,0:T(8,128)(2,1)} %fusion.37), channel_id=1, source_target_pairs={{0,2},{1,3},{2,0},{3,1},{4,6},{5,7},{6,4},{7,5},{8,10},{9,11},{10,... | collective-permute-start | bytes 294920 | tf_op jit(solution)/shard_map/ppermute | solution.py:10
  19.1 5.0 %collective-permute-start.1 = (bf16[128,384]{1,0:T(8,128)(2,1)}, bf16[128,384]{1,0:T(8,128)(2,1)}, u32[]{:S(2)}, u32[]{:S(2)}) collective-permute-start(bf16[128,384]{1,0:T(8,128)(2,1)} %fusion.34), channel_id=1, source_target_pairs={{0,2},{1,3},{2,0},{3,1},{4,6},{5,7},{6,4},{7,5},{8,10},{9,11},{10,... | collective-permute-start | bytes 294920 | tf_op jit(solution)/shard_map/ppermute | solution.py:10
  19.2 2.6 %copy-start.24 = (bf16[128,384]{0,1:T(8,128)(2,1)}, bf16[128,384]{0,1:T(8,128)(2,1)S(1)}, u32[]{:S(2)}) copy-start(bf16[128,384]{0,1:T(8,128)(2,1)S(1)} %copy.299) | copy-start | bytes 294916
  19.6 2.1 %copy-start.26 = (bf16[128,384]{0,1:T(8,128)(2,1)}, bf16[128,384]{0,1:T(8,128)(2,1)S(1)}, u32[]{:S(2)}) copy-start(bf16[128,384]{0,1:T(8,128)(2,1)S(1)} %copy.321) | copy-start | bytes 294916
  20.8 1.0 copy-start.37
  22.9 12.4 %collective-permute-start.5 = (bf16[128,384]{1,0:T(8,128)(2,1)}, bf16[128,384]{1,0:T(8,128)(2,1)}, u32[]{:S(2)}, u32[]{:S(2)}) collective-permute-start(bf16[128,384]{1,0:T(8,128)(2,1)} %bitcast.146), channel_id=1, source_target_pairs={{0,4},{1,5},{2,6},{3,7},{4,0},{5,1},{6,2},{7,3},{8,12},{9,13},{10,... | collective-permute-start | bytes 294920 | tf_op jit(solution)/shard_map/ppermute | solution.py:10
  25.3 4.3 %copy-start.35 = (bf16[32,6,64]{2,1,0:T(8,128)(2,1)S(1)}, bf16[32,6,64]{2,1,0:T(8,128)(2,1)}, u32[]{:S(2)}) copy-start(bf16[32,6,64]{2,1,0:T(8,128)(2,1)} %convert_element_type.251) | copy-start | bytes 73732
  25.6 3.8 %collective-permute-start.2 = (bf16[128,384]{1,0:T(8,128)(2,1)S(1)}, bf16[128,384]{1,0:T(8,128)(2,1)S(1)}, u32[]{:S(2)}, u32[]{:S(2)}) collective-permute-start(bf16[128,384]{1,0:T(8,128)(2,1)S(1)} %fusion.35), channel_id=1, source_target_pairs={{0,4},{1,5},{2,6},{3,7},{4,0},{5,1},{6,2},{7,3},{8,12},{9,13},{10,... | collective-permute-start | bytes 294920 | tf_op jit(solution)/shard_map/ppermute | solution.py:10
  27.1 3.4 %copy-start.14 = (bf16[128,384]{0,1:T(8,128)(2,1)}, bf16[128,384]{0,1:T(8,128)(2,1)S(1)}, u32[]{:S(2)}) copy-start(bf16[128,384]{0,1:T(8,128)(2,1)S(1)} %copy.302) | copy-start | bytes 294916
  28.4 0.9 copy-start.20
  29.5 1.0 copy-start.16
  29.8 6.5 %copy-start.7 = (f32[6,32,128]{2,1,0:T(8,128)}, f32[6,32,128]{2,1,0:T(8,128)S(1)}, u32[]{:S(2)}) copy-start(f32[6,32,128]{2,1,0:T(8,128)S(1)} %get-tuple-element.37) | copy-start | bytes 294916
  32.6 4.2 %copy-start.38 = (f32[64,384]{1,0:T(8,128)S(1)}, f32[64,384]{1,0:T(8,128)}, u32[]{:S(2)}) copy-start(f32[64,384]{1,0:T(8,128)} %copy.328) | copy-start | bytes 294916
  36.3 0.7 copy-start.18
  40.5 2.3 %copy-start.5 = (bf16[1,256,384]{1,2,0:T(8,128)(2,1)S(1)}, bf16[1,256,384]{1,2,0:T(8,128)(2,1)}, u32[]{:S(2)}) copy-start(bf16[1,256,384]{1,2,0:T(8,128)(2,1)} %copy.316) | copy-start | bytes 589828
  40.5 2.3 %copy-start.10 = (f32[256,384]{0,1:T(8,128)S(1)}, f32[256,384]{0,1:T(8,128)}, u32[]{:S(2)}) copy-start(f32[256,384]{0,1:T(8,128)} %copy.317) | copy-start | bytes 1179652
  41.6 1.1 copy-start.11
  42.8 1.8 copy-start.41
  43.7 1.2 copy-start.4
  44.6 1.0 copy-start.2
  45.0 0.9 copy-start.33
  45.9 1.7 copy-start.6
  47.6 2.7 %copy-start.34 = (f32[256,6]{1,0:T(8,128)S(1)}, f32[256,6]{1,0:T(8,128)}, u32[]{:S(2)}) copy-start(f32[256,6]{1,0:T(8,128)} %copy.335) | copy-start | bytes 18436
  47.6 3.4 %copy-start.8 = (f32[6,32,128]{2,1,0:T(8,128)S(1)}, f32[6,32,128]{2,1,0:T(8,128)}, u32[]{:S(2)}) copy-start(f32[6,32,128]{2,1,0:T(8,128)} %copy-done.7) | copy-start | bytes 294916
  47.6 3.7 %copy-start.19 = (bf16[128,384]{0,1:T(8,128)(2,1)S(1)}, bf16[128,384]{0,1:T(8,128)(2,1)}, u32[]{:S(2)}) copy-start(bf16[128,384]{0,1:T(8,128)(2,1)} %copy-done.18) | copy-start | bytes 294916
  49.3 2.2 %copy-start.17 = (bf16[128,384]{0,1:T(8,128)(2,1)S(1)}, bf16[128,384]{0,1:T(8,128)(2,1)}, u32[]{:S(2)}) copy-start(bf16[128,384]{0,1:T(8,128)(2,1)} %copy-done.16) | copy-start | bytes 294916
  49.3 2.3 %copy-start.36 = (bf16[32,6,64]{2,1,0:T(8,128)(2,1)S(1)}, bf16[32,6,64]{2,1,0:T(8,128)(2,1)}, u32[]{:S(2)}) copy-start(bf16[32,6,64]{2,1,0:T(8,128)(2,1)} %convert_element_type.251) | copy-start | bytes 73732
  50.3 2.0 copy-start.27
  50.8 1.8 copy-start.23
  51.3 1.6 copy-start.25
  52.0 3.5 %copy-start.21 = (bf16[128,384]{0,1:T(8,128)(2,1)S(1)}, bf16[128,384]{0,1:T(8,128)(2,1)}, u32[]{:S(2)}) copy-start(bf16[128,384]{0,1:T(8,128)(2,1)} %copy-done.20) | copy-start | bytes 294916
  52.3 3.5 %copy-start.13 = (bf16[64,384]{0,1:T(8,128)(2,1)S(1)}, bf16[64,384]{0,1:T(8,128)(2,1)}, u32[]{:S(2)}) copy-start(bf16[64,384]{0,1:T(8,128)(2,1)} %copy-done.12) | copy-start | bytes 147460
  52.3 3.7 %copy-start.15 = (bf16[128,384]{0,1:T(8,128)(2,1)S(1)}, bf16[128,384]{0,1:T(8,128)(2,1)}, u32[]{:S(2)}) copy-start(bf16[128,384]{0,1:T(8,128)(2,1)} %copy-done.14) | copy-start | bytes 294916
  52.6 3.6 %copy-start.9 = (f32[6,64,256]{2,1,0:T(8,128)S(1)}, f32[6,64,256]{2,1,0:T(8,128)}, u32[]{:S(2)}) copy-start(f32[6,64,256]{2,1,0:T(8,128)} %fusion.16) | copy-start | bytes 1179652
  56.5 3.4 %copy-start.32 = (f32[6,64,128]{2,1,0:T(8,128)S(1)}, f32[6,64,128]{2,1,0:T(8,128)}, u32[]{:S(2)}) copy-start(f32[6,64,128]{2,1,0:T(8,128)} %fusion.44) | copy-start | bytes 589828
  58.8 2.2 %copy-start.31 = (f32[6,64,128]{2,1,0:T(8,128)S(1)}, f32[6,64,128]{2,1,0:T(8,128)}, u32[]{:S(2)}) copy-start(f32[6,64,128]{2,1,0:T(8,128)} %fusion.68) | copy-start | bytes 589828
  61.6 12.5 %copy-start.39 = (f32[128,384]{1,0:T(8,128)S(1)}, f32[128,384]{1,0:T(8,128)}, u32[]{:S(2)}) copy-start(f32[128,384]{1,0:T(8,128)} %copy.357) | copy-start | bytes 589828
  62.3 129.0 %collective-permute-start.8 = (f32[128,384]{1,0:T(8,128)S(1)}, f32[128,384]{1,0:T(8,128)}, u32[]{:S(2)}, u32[]{:S(2)}) collective-permute-start(f32[128,384]{1,0:T(8,128)S(1)} %copy.351), channel_id=1, source_target_pairs={{0,2},{1,3},{2,0},{3,1},{4,6},{5,7},{6,4},{7,5},{8,10},{9,11},{10,... | collective-permute-start | bytes 589832 | tf_op jit(solution)/shard_map/ppermute | solution.py:10
  64.7 135.6 %collective-permute-start.10 = (f32[128,384]{1,0:T(8,128)S(1)}, f32[128,384]{1,0:T(8,128)}, u32[]{:S(2)}, u32[]{:S(2)}) collective-permute-start(f32[128,384]{1,0:T(8,128)S(1)} %copy.353), channel_id=1, source_target_pairs={{0,1},{1,0},{2,3},{3,2},{4,5},{5,4},{6,7},{7,6},{8,9},{9,8},{10,11... | collective-permute-start | bytes 589832 | tf_op jit(solution)/shard_map/ppermute | solution.py:10
  67.0 134.6 %collective-permute-start.15 = (f32[128,384]{1,0:T(8,128)S(1)}, f32[128,384]{1,0:T(8,128)S(1)}, u32[]{:S(2)}, u32[]{:S(2)}) collective-permute-start(f32[128,384]{1,0:T(8,128)S(1)} %copy.361), channel_id=1, source_target_pairs={{0,1},{1,0},{2,3},{3,2},{4,5},{5,4},{6,7},{7,6},{8,9},{9,8},{10,11... | collective-permute-start | bytes 589832 | tf_op jit(solution)/shard_map/ppermute | solution.py:10
  67.0 7.1 %collective-permute-start.6 = (f32[128,384]{1,0:T(8,128)}, f32[128,384]{1,0:T(8,128)S(1)}, u32[]{:S(2)}, u32[]{:S(2)}) collective-permute-start(f32[128,384]{1,0:T(8,128)} %copy.349), channel_id=1, source_target_pairs={{0,4},{1,5},{2,6},{3,7},{4,0},{5,1},{6,2},{7,3},{8,12},{9,13},{10,... | collective-permute-start | bytes 589832 | tf_op jit(solution)/shard_map/ppermute | solution.py:10
  67.5 126.9 %collective-permute-start.13 = (f32[128,384]{1,0:T(8,128)S(1)}, f32[128,384]{1,0:T(8,128)}, u32[]{:S(2)}, u32[]{:S(2)}) collective-permute-start(f32[128,384]{1,0:T(8,128)S(1)} %copy.359), channel_id=1, source_target_pairs={{0,2},{1,3},{2,0},{3,1},{4,6},{5,7},{6,4},{7,5},{8,10},{9,11},{10,... | collective-permute-start | bytes 589832 | tf_op jit(solution)/shard_map/ppermute | solution.py:10
  74.1 5.6 %collective-permute-start.11 = (f32[128,384]{1,0:T(8,128)S(1)}, f32[128,384]{1,0:T(8,128)S(1)}, u32[]{:S(2)}, u32[]{:S(2)}) collective-permute-start(f32[128,384]{1,0:T(8,128)S(1)} %copy-done.39), channel_id=1, source_target_pairs={{0,4},{1,5},{2,6},{3,7},{4,0},{5,1},{6,2},{7,3},{8,12},{9,13},{10,... | collective-permute-start | bytes 589832 | tf_op jit(solution)/shard_map/ppermute | solution.py:10
  79.8 112.6 %collective-permute-start.7 = (f32[128,384]{1,0:T(8,128)S(1)}, f32[128,384]{1,0:T(8,128)S(1)}, u32[]{:S(2)}, u32[]{:S(2)}) collective-permute-start(f32[128,384]{1,0:T(8,128)S(1)} %select_n.151), channel_id=1, source_target_pairs={{0,2},{1,3},{2,0},{3,1},{4,6},{5,7},{6,4},{7,5},{8,10},{9,11},{10,... | collective-permute-start | bytes 589832 | tf_op jit(solution)/shard_map/ppermute | solution.py:10
  191.3 6.4 %collective-permute-start.12 = (f32[128,384]{1,0:T(8,128)S(1)}, f32[128,384]{1,0:T(8,128)}, u32[]{:S(2)}, u32[]{:S(2)}) collective-permute-start(f32[128,384]{1,0:T(8,128)S(1)} %select_n.159), channel_id=1, source_target_pairs={{0,2},{1,3},{2,0},{3,1},{4,6},{5,7},{6,4},{7,5},{8,10},{9,11},{10,... | collective-permute-start | bytes 589832 | tf_op jit(solution)/shard_map/ppermute | solution.py:10
  193.8 6.4 %collective-permute-start.9 = (f32[128,384]{1,0:T(8,128)S(1)}, f32[128,384]{1,0:T(8,128)S(1)}, u32[]{:S(2)}, u32[]{:S(2)}) collective-permute-start(f32[128,384]{1,0:T(8,128)S(1)} %select_n.155), channel_id=1, source_target_pairs={{0,1},{1,0},{2,3},{3,2},{4,5},{5,4},{6,7},{7,6},{8,9},{9,8},{10,11... | collective-permute-start | bytes 589832 | tf_op jit(solution)/shard_map/ppermute | solution.py:10
  199.2 2.5 %collective-permute-start.14 = (f32[128,384]{1,0:T(8,128)S(1)}, f32[128,384]{1,0:T(8,128)S(1)}, u32[]{:S(2)}, u32[]{:S(2)}) collective-permute-start(f32[128,384]{1,0:T(8,128)S(1)} %select_n.163), channel_id=1, source_target_pairs={{0,1},{1,0},{2,3},{3,2},{4,5},{5,4},{6,7},{7,6},{8,9},{9,8},{10,11... | collective-permute-start | bytes 589832 | tf_op jit(solution)/shard_map/ppermute | solution.py:10
Sparse Core Ops, SparseCore 0:
  59.0 130.6 all-reduce.1
where the time goes:
time: 211 us; the launch traced here: 210 us
  waiting for transfers between devices  125 us (59%)
  local copies, waits for them, and re-layouts  32.4 us (15%)
  between operations  15.4 us (7%)
  other arithmetic  12.8 us (6%)
  starting transfers between devices  12.6 us (6%)
  matrix products  12.6 us (6%)
    psum x1, waiting for transfers between devices, shards(): summed = lax.psum(weight_term, ('dp', 'seqhi', 'seqlo'))  109 us
    ppermute x16, waiting for transfers between devices, swapped(): return lax.ppermute(value, axis, pairs)  15.3 us
    ppermute x16, starting transfers between devices, swapped(): return lax.ppermute(value, axis, pairs)  12.6 us
  transfers between devices with their start and end apart: 17, of which 5 were waited for; matrix products, arithmetic and copies ran while one was open for 14% of the time, Pallas kernels for 0%

commit v1 on v0

--- a/solution.py
+++ b/solution.py
@@ -152,7 +152,9 @@
     weight_term = lax.dot_general(
         attended, cotan_local, (((0,), (0,)), ((), ())), preferred_element_type=jnp.float32
     )
-    summed = lax.psum(weight_term, ("dp", "seqhi", "seqlo"))
+    summed = weight_term
+    for mesh_axis in (("seqhi", "seqlo"), "dp"):
+        summed = lax.psum(summed, mesh_axis)
     weight_gradient = lax.dynamic_slice_in_dim(summed, lax.axis_index("dp") * own_rows, own_rows, 0)
     backward = lax.dot_general(
         cotan_local, out_weight, (((1,), (1,)), ((), ())), preferred_element_type=jnp.float32

time: 211 us -> 168 us (0.80)
  waiting for transfers between devices: 125 us -> 78.2 us
  starting transfers between devices: 12.6 us -> 15.3 us
    psum x1 -> x2, waiting for transfers between devices: 109 us -> 64.6 us  [shards(): summed = lax.psum(summed, mesh_axis)]
    ppermute x16, starting transfers between devices: 12.6 us -> 15.2 us  [swapped(): return lax.ppermute(value, axis, pairs)]
  transfers between devices with their start and end apart: 17 -> 18, of which waited for: 5 -> 7; matrix products, arithmetic and copies ran while one was open for 14% -> 18% of each run, Pallas kernels for 0% -> 0%
where the time goes in v1:
time: 168 us; the launch traced here: 167 us
  waiting for transfers between devices  78.2 us (47%)
  local copies, waits for them, and re-layouts  32.4 us (19%)
  between operations  15.4 us (9%)
  starting transfers between devices  15.3 us (9%)
  other arithmetic  12.8 us (8%)
  matrix products  12.6 us (8%)
    psum x2, waiting for transfers between devices, shards(): summed = lax.psum(summed, mesh_axis)  64.6 us
    ppermute x16, starting transfers between devices, swapped(): return lax.ppermute(value, axis, pairs)  15.2 us
    ppermute x16, waiting for transfers between devices, swapped(): return lax.ppermute(value, axis, pairs)  13.6 us
    reshape x12, local copies, waits for them, and re-layouts, spread_rows(): return widened.reshape((matrix.shape[0] * factor,) + matrix.shape[1:])  3.99 us
    ppermute x6, local copies, waits for them, and re-layouts, swapped(): return lax.ppermute(value, axis, pairs)  3.39 us
  transfers between devices with their start and end apart: 18, of which 7 were waited for; matrix products, arithmetic and copies ran while one was open for 18% of the time, Pallas kernels for 0%

profile of v1, /device:TPU:1, one launch (start us, length us, event | category | flops | bytes accessed | tf_op | source)
XLA Modules:
  0.0 166.8 jit_solution(9592152932415819783)
XLA Ops:
  7.2 1.2 reshape.433
  8.5 0.3 fusion.63
  9.1 0.3 fusion.59
  9.5 0.5 collective-permute-start.3
  10.2 0.8 copy.316
  11.4 0.3 fusion.60
  12.0 0.4 convert_reduce_fusion.1
  12.9 0.4 fusion.67
  13.5 0.7 convert_element_type.251
  14.9 0.7 fusion.37
  15.5 2.3 %collective-permute-start.4 = (bf16[128,384]{1,0:T(8,128)(2,1)}, bf16[128,384]{1,0:T(8,128)(2,1)S(1)}, u32[]{:S(2)}, u32[]{:S(2)}) collective-permute-start(bf16[128,384]{1,0:T(8,128)(2,1)} %fusion.37), channel_id=1, source_target_pairs={{0,2},{1,3},{2,0},{3,1},{4,6},{5,7},{6,4},{7,5},{8,10},{9,11},{10,... | collective-permute-start | bytes 294920 | tf_op jit(solution)/shard_map/ppermute | solution.py:10
  18.4 0.7 fusion.34
  20.0 0.8 collective-permute-done.4
  20.8 1.0 broadcast_select_fusion.1
  22.3 0.6 copy.454
  22.9 1.1 collective-permute-start.5
  24.0 1.0 broadcast_select_fusion.3
  25.6 0.4 collective-permute-start.2
  26.1 1.0 copy.302
  27.1 0.3 fusion.65
  27.4 1.0 copy.325
  28.6 0.8 copy.328
  30.7 1.9 %divide_convert_fusion = (bf16[256,384]{1,0:T(8,128)(2,1)}, f32[256,384]{1,0:T(8,128)S(1)}) fusion(f32[256,384]{1,0:T(8,128)S(1)} %copy.314, bf16[384,384]{1,0:T(8,128)(2,1)S(1)} %copy-done, bf16[1,256,384]{2,1,0:T(8,128)(2,1)} %param.11), kind=kOutput, calls=%fused_computation.35 | convolution fusion | flops 75890688 | bytes 1474560 | tf_op jit(solution)/shard_map/dot_general | solution.py:159
  32.6 0.8 copy.388
  33.4 0.9 copy.317
  34.3 1.0 reshape.442
  35.3 1.0 copy.326
  37.1 0.9 broadcast_in_dim.46
  38.0 1.5 reshape.410
  39.5 1.0 copy.330
  40.5 1.1 copy.315
  41.7 1.1 fusion.16
  42.8 1.0 fusion.57
  43.7 0.8 copy.335
  44.6 0.4 multiply_convert_fusion
  45.0 0.4 fusion.70
  45.9 0.3 div.50.clone
  46.2 1.4 div.55
  47.6 1.6 divide_reduce_fusion
  49.7 0.6 convert_element_type.281
  52.8 0.9 fusion.68
  53.8 0.9 copy.390
  54.7 0.8 fusion.44
  56.7 2.1 %fusion.30 = f32[384,384]{1,0:T(8,128)} fusion(bf16[256,384]{0,1:T(8,128)(2,1)} %bitcast.190, bf16[1,256,384]{2,1,0:T(8,128)(2,1)} %param.11), kind=kOutput, calls=%fused_computation.59 | convolution fusion | flops 75497472 | bytes 983040 | tf_op jit(solution)/shard_map/dot_general | solution.py:152
  59.1 0.8 copy.357
  60.1 0.8 copy.349
  62.3 2.4 %collective-permute-start.8 = (f32[128,384]{1,0:T(8,128)S(1)}, f32[128,384]{1,0:T(8,128)}, u32[]{:S(2)}, u32[]{:S(2)}) collective-permute-start(f32[128,384]{1,0:T(8,128)S(1)} %copy.351), channel_id=1, source_target_pairs={{0,2},{1,3},{2,0},{3,1},{4,6},{5,7},{6,4},{7,5},{8,10},{9,11},{10,... | collective-permute-start | bytes 589832 | tf_op jit(solution)/shard_map/ppermute | solution.py:10
  64.7 2.4 %collective-permute-start.10 = (f32[128,384]{1,0:T(8,128)S(1)}, f32[128,384]{1,0:T(8,128)}, u32[]{:S(2)}, u32[]{:S(2)}) collective-permute-start(f32[128,384]{1,0:T(8,128)S(1)} %copy.353), channel_id=1, source_target_pairs={{0,1},{1,0},{2,3},{3,2},{4,5},{5,4},{6,7},{7,6},{8,9},{9,8},{10,11... | collective-permute-start | bytes 589832 | tf_op jit(solution)/shard_map/ppermute | solution.py:10
  67.1 0.5 collective-permute-start.6
  67.6 0.7 add_convert_fusion.2
  68.3 7.0 %collective-permute-done.6 = f32[128,384]{1,0:T(8,128)S(1)} collective-permute-done((f32[128,384]{1,0:T(8,128)}, f32[128,384]{1,0:T(8,128)S(1)}, u32[]{:S(2)}, u32[]{:S(2)}) %collective-permute-start.6) | collective-permute-done | bytes 196640 | tf_op jit(solution)/shard_map/ppermute | solution.py:10
  75.7 5.1 %collective-permute-done.11 = f32[128,384]{1,0:T(8,128)S(1)} collective-permute-done((f32[128,384]{1,0:T(8,128)S(1)}, f32[128,384]{1,0:T(8,128)S(1)}, u32[]{:S(2)}, u32[]{:S(2)}) %collective-permute-start.11) | collective-permute-done | bytes 196640 | tf_op jit(solution)/shard_map/ppermute | solution.py:10
  81.3 35.5 %all-reduce.3.cloned.1.call-done = f32[384,384]{1,0:T(8,128)} async-done(((f32[384,384]{1,0:T(8,128)}), f32[384,384]{1,0:T(8,128)}) %all-reduce.3.cloned.1.call-update) | async-done | bytes 589840 | tf_op jit(solution)/shard_map/psum | solution.py:157
  116.8 0.5 collective-permute-start.12
  117.3 1.0 add_multiply_fusion.1
  118.7 2.1 %collective-permute-start.9 = (f32[128,384]{1,0:T(8,128)S(1)}, f32[128,384]{1,0:T(8,128)S(1)}, u32[]{:S(2)}, u32[]{:S(2)}) collective-permute-start(f32[128,384]{1,0:T(8,128)S(1)} %select_n.155), channel_id=1, source_target_pairs={{0,1},{1,0},{2,3},{3,2},{4,5},{5,4},{6,7},{7,6},{8,9},{9,8},{10,11... | collective-permute-start | bytes 589832 | tf_op jit(solution)/shard_map/ppermute | solution.py:10
  120.8 0.7 collective-permute-done.12
  121.5 1.1 add_add_fusion.1
  123.0 2.9 %collective-permute-start.14 = (f32[128,384]{1,0:T(8,128)S(1)}, f32[128,384]{1,0:T(8,128)S(1)}, u32[]{:S(2)}, u32[]{:S(2)}) collective-permute-start(f32[128,384]{1,0:T(8,128)S(1)} %select_n.163), channel_id=1, source_target_pairs={{0,1},{1,0},{2,3},{3,2},{4,5},{5,4},{6,7},{7,6},{8,9},{9,8},{10,11... | collective-permute-start | bytes 589832 | tf_op jit(solution)/shard_map/ppermute | solution.py:10
  125.9 1.0 add_multiply_fusion
  127.9 0.7 add_convert_fusion.1
  128.6 0.7 add_convert_fusion
  129.3 29.1 %all-reduce.5.cloned.1.call-done = f32[384,384]{1,0:T(8,128)} async-done(((f32[384,384]{1,0:T(8,128)}), f32[384,384]{1,0:T(8,128)}) %all-reduce.5.cloned.1.call-update) | async-done | bytes 589840 | tf_op jit(solution)/shard_map/psum | solution.py:157
  158.4 1.6 constant_dynamic-slice_fusion
  (241 shorter events, 15.8 us)
Async XLA Ops:
  7.2 23.5 %copy-start = (bf16[384,384]{1,0:T(8,128)(2,1)S(1)}, bf16[384,384]{1,0:T(8,128)(2,1)}, u32[]{:S(2)}) copy-start(bf16[384,384]{1,0:T(8,128)(2,1)} %param.10) | copy-start | bytes 884740
  7.2 1.8 %copy-start.29 = (bf16[1,256,384]{2,1,0:T(8,128)(2,1)S(1)}, bf16[1,256,384]{2,1,0:T(8,128)(2,1)}, u32[]{:S(2)}) copy-start(bf16[1,256,384]{2,1,0:T(8,128)(2,1)} %param.8) | copy-start | bytes 589828
  7.2 109.5 %all-reduce.3.cloned.1.call-start = ((), (), s32[]{:S(2)}) async-start(), calls=%async_computation | async-start | bytes 1179648 | tf_op jit(solution)/shard_map/psum | solution.py:157
  8.4 1.6 copy-start.28
  8.8 2.2 %copy-start.30 = (bf16[1,256,384]{2,1,0:T(8,128)(2,1)S(1)}, bf16[1,256,384]{2,1,0:T(8,128)(2,1)}, u32[]{:S(2)}) copy-start(bf16[1,256,384]{2,1,0:T(8,128)(2,1)} %param.6) | copy-start | bytes 589828
  8.8 5.4 %collective-permute-start = (bf16[128,384]{1,0:T(8,128)(2,1)S(1)}, bf16[128,384]{1,0:T(8,128)(2,1)S(1)}, u32[]{:S(2)}, u32[]{:S(2)}) collective-permute-start(bf16[128,384]{1,0:T(8,128)(2,1)S(1)} %fusion.33), channel_id=1, source_target_pairs={{0,1},{1,0},{2,3},{3,2},{4,5},{5,4},{6,7},{7,6},{8,9},{9,8},{10,11... | collective-permute-start | bytes 294920 | tf_op jit(solution)/shard_map/ppermute | solution.py:10
  9.5 4.7 %collective-permute-start.3 = (bf16[128,384]{1,0:T(8,128)(2,1)S(1)}, bf16[128,384]{1,0:T(8,128)(2,1)S(1)}, u32[]{:S(2)}, u32[]{:S(2)}) collective-permute-start(bf16[128,384]{1,0:T(8,128)(2,1)S(1)} %fusion.36), channel_id=1, source_target_pairs={{0,1},{1,0},{2,3},{3,2},{4,5},{5,4},{6,7},{7,6},{8,9},{9,8},{10,11... | collective-permute-start | bytes 294920 | tf_op jit(solution)/shard_map/ppermute | solution.py:10
  10.2 2.7 %copy-start.1 = (bf16[1,256,384]{1,2,0:T(8,128)(2,1)}, bf16[1,256,384]{1,2,0:T(8,128)(2,1)S(1)}, u32[]{:S(2)}) copy-start(bf16[1,256,384]{1,2,0:T(8,128)(2,1)S(1)} %copy.293) | copy-start | bytes 589828
  10.2 1.8 %copy-start.42 = (f32[6]{0:T(128)S(1)}, f32[6]{0:T(128)}, u32[]{:S(2)}) copy-start(f32[6]{0:T(128)} %param.9) | copy-start | bytes 76
  11.2 1.7 %copy-start.3 = (bf16[1,256,384]{1,2,0:T(8,128)(2,1)}, bf16[1,256,384]{1,2,0:T(8,128)(2,1)S(1)}, u32[]{:S(2)}) copy-start(bf16[1,256,384]{1,2,0:T(8,128)(2,1)S(1)} %copy.292) | copy-start | bytes 589828
  11.8 7.4 %copy-start.22 = (bf16[128,1,384]{0,2,1:T(8,128)(2,1)}, bf16[128,1,384]{0,2,1:T(8,128)(2,1)S(1)}, u32[]{:S(2)}) copy-start(bf16[128,1,384]{0,2,1:T(8,128)(2,1)S(1)} %copy.296) | copy-start | bytes 294916
  12.0 17.5 %copy-start.40 = (f32[6]{0:T(128)}, f32[6]{0:T(128)S(1)}, u32[]{:S(2)}) copy-start(f32[6]{0:T(128)S(1)} %broadcast_multiply_fusion.1) | copy-start | bytes 76
  12.5 14.6 %copy-start.12 = (bf16[64,384]{0,1:T(8,128)(2,1)}, bf16[64,384]{0,1:T(8,128)(2,1)S(1)}, u32[]{:S(2)}) copy-start(bf16[64,384]{0,1:T(8,128)(2,1)S(1)} %copy.389) | copy-start | bytes 147460
  15.5 5.3 %collective-permute-start.4 = (bf16[128,384]{1,0:T(8,128)(2,1)}, bf16[128,384]{1,0:T(8,128)(2,1)S(1)}, u32[]{:S(2)}, u32[]{:S(2)}) collective-permute-start(bf16[128,384]{1,0:T(8,128)(2,1)} %fusion.37), channel_id=1, source_target_pairs={{0,2},{1,3},{2,0},{3,1},{4,6},{5,7},{6,4},{7,5},{8,10},{9,11},{10,... | collective-permute-start | bytes 294920 | tf_op jit(solution)/shard_map/ppermute | solution.py:10
  19.1 5.0 %collective-permute-start.1 = (bf16[128,384]{1,0:T(8,128)(2,1)}, bf16[128,384]{1,0:T(8,128)(2,1)}, u32[]{:S(2)}, u32[]{:S(2)}) collective-permute-start(bf16[128,384]{1,0:T(8,128)(2,1)} %fusion.34), channel_id=1, source_target_pairs={{0,2},{1,3},{2,0},{3,1},{4,6},{5,7},{6,4},{7,5},{8,10},{9,11},{10,... | collective-permute-start | bytes 294920 | tf_op jit(solution)/shard_map/ppermute | solution.py:10
  19.2 2.6 %copy-start.24 = (bf16[128,384]{0,1:T(8,128)(2,1)}, bf16[128,384]{0,1:T(8,128)(2,1)S(1)}, u32[]{:S(2)}) copy-start(bf16[128,384]{0,1:T(8,128)(2,1)S(1)} %copy.299) | copy-start | bytes 294916
  19.6 2.1 %copy-start.26 = (bf16[128,384]{0,1:T(8,128)(2,1)}, bf16[128,384]{0,1:T(8,128)(2,1)S(1)}, u32[]{:S(2)}) copy-start(bf16[128,384]{0,1:T(8,128)(2,1)S(1)} %copy.321) | copy-start | bytes 294916
  20.8 1.0 copy-start.37
  22.9 12.4 %collective-permute-start.5 = (bf16[128,384]{1,0:T(8,128)(2,1)}, bf16[128,384]{1,0:T(8,128)(2,1)}, u32[]{:S(2)}, u32[]{:S(2)}) collective-permute-start(bf16[128,384]{1,0:T(8,128)(2,1)} %bitcast.146), channel_id=1, source_target_pairs={{0,4},{1,5},{2,6},{3,7},{4,0},{5,1},{6,2},{7,3},{8,12},{9,13},{10,... | collective-permute-start | bytes 294920 | tf_op jit(solution)/shard_map/ppermute | solution.py:10
  25.3 4.3 %copy-start.35 = (bf16[32,6,64]{2,1,0:T(8,128)(2,1)S(1)}, bf16[32,6,64]{2,1,0:T(8,128)(2,1)}, u32[]{:S(2)}) copy-start(bf16[32,6,64]{2,1,0:T(8,128)(2,1)} %convert_element_type.251) | copy-start | bytes 73732
  25.6 3.8 %collective-permute-start.2 = (bf16[128,384]{1,0:T(8,128)(2,1)S(1)}, bf16[128,384]{1,0:T(8,128)(2,1)S(1)}, u32[]{:S(2)}, u32[]{:S(2)}) collective-permute-start(bf16[128,384]{1,0:T(8,128)(2,1)S(1)} %fusion.35), channel_id=1, source_target_pairs={{0,4},{1,5},{2,6},{3,7},{4,0},{5,1},{6,2},{7,3},{8,12},{9,13},{10,... | collective-permute-start | bytes 294920 | tf_op jit(solution)/shard_map/ppermute | solution.py:10
  27.1 3.4 %copy-start.14 = (bf16[128,384]{0,1:T(8,128)(2,1)}, bf16[128,384]{0,1:T(8,128)(2,1)S(1)}, u32[]{:S(2)}) copy-start(bf16[128,384]{0,1:T(8,128)(2,1)S(1)} %copy.302) | copy-start | bytes 294916
  28.4 0.9 copy-start.20
  29.5 1.0 copy-start.16
  29.8 6.5 %copy-start.7 = (f32[6,32,128]{2,1,0:T(8,128)}, f32[6,32,128]{2,1,0:T(8,128)S(1)}, u32[]{:S(2)}) copy-start(f32[6,32,128]{2,1,0:T(8,128)S(1)} %get-tuple-element.37) | copy-start | bytes 294916
  32.6 4.2 %copy-start.38 = (f32[64,384]{1,0:T(8,128)S(1)}, f32[64,384]{1,0:T(8,128)}, u32[]{:S(2)}) copy-start(f32[64,384]{1,0:T(8,128)} %copy.328) | copy-start | bytes 294916
  36.3 0.7 copy-start.18
  40.5 2.3 %copy-start.5 = (bf16[1,256,384]{1,2,0:T(8,128)(2,1)S(1)}, bf16[1,256,384]{1,2,0:T(8,128)(2,1)}, u32[]{:S(2)}) copy-start(bf16[1,256,384]{1,2,0:T(8,128)(2,1)} %copy.316) | copy-start | bytes 589828
  40.5 2.3 %copy-start.10 = (f32[256,384]{0,1:T(8,128)S(1)}, f32[256,384]{0,1:T(8,128)}, u32[]{:S(2)}) copy-start(f32[256,384]{0,1:T(8,128)} %copy.317) | copy-start | bytes 1179652
  41.6 1.1 copy-start.11
  42.8 1.8 %copy-start.41 = (f32[6]{0:T(128)S(1)}, f32[6]{0:T(128)}, u32[]{:S(2)}) copy-start(f32[6]{0:T(128)} %copy-done.40) | copy-start | bytes 76
  43.7 1.2 copy-start.4
  44.6 1.0 copy-start.2
  45.0 0.9 copy-start.33
  45.9 1.7 %copy-start.6 = (f32[128,2,384]{2,1,0:T(2,128)S(1)}, f32[128,2,384]{2,1,0:T(2,128)}, u32[]{:S(2)}) copy-start(f32[128,2,384]{2,1,0:T(2,128)} %reshape.442) | copy-start | bytes 1179652
  47.6 2.7 %copy-start.34 = (f32[256,6]{1,0:T(8,128)S(1)}, f32[256,6]{1,0:T(8,128)}, u32[]{:S(2)}) copy-start(f32[256,6]{1,0:T(8,128)} %copy.335) | copy-start | bytes 18436
  47.6 3.4 %copy-start.8 = (f32[6,32,128]{2,1,0:T(8,128)S(1)}, f32[6,32,128]{2,1,0:T(8,128)}, u32[]{:S(2)}) copy-start(f32[6,32,128]{2,1,0:T(8,128)} %copy-done.7) | copy-start | bytes 294916
  47.6 3.7 %copy-start.19 = (bf16[128,384]{0,1:T(8,128)(2,1)S(1)}, bf16[128,384]{0,1:T(8,128)(2,1)}, u32[]{:S(2)}) copy-start(bf16[128,384]{0,1:T(8,128)(2,1)} %copy-done.18) | copy-start | bytes 294916
  49.3 2.2 %copy-start.17 = (bf16[128,384]{0,1:T(8,128)(2,1)S(1)}, bf16[128,384]{0,1:T(8,128)(2,1)}, u32[]{:S(2)}) copy-start(bf16[128,384]{0,1:T(8,128)(2,1)} %copy-done.16) | copy-start | bytes 294916
  49.3 2.3 %copy-start.36 = (bf16[32,6,64]{2,1,0:T(8,128)(2,1)S(1)}, bf16[32,6,64]{2,1,0:T(8,128)(2,1)}, u32[]{:S(2)}) copy-start(bf16[32,6,64]{2,1,0:T(8,128)(2,1)} %convert_element_type.251) | copy-start | bytes 73732
  50.3 2.0 %copy-start.27 = (bf16[128,384]{0,1:T(8,128)(2,1)S(1)}, bf16[128,384]{0,1:T(8,128)(2,1)}, u32[]{:S(2)}) copy-start(bf16[128,384]{0,1:T(8,128)(2,1)} %copy-done.26) | copy-start | bytes 294916
  50.8 1.8 %copy-start.23 = (bf16[128,1,384]{0,2,1:T(8,128)(2,1)S(1)}, bf16[128,1,384]{0,2,1:T(8,128)(2,1)}, u32[]{:S(2)}) copy-start(bf16[128,1,384]{0,2,1:T(8,128)(2,1)} %copy-done.22) | copy-start | bytes 294916
  51.3 1.6 copy-start.25
  52.0 3.5 %copy-start.21 = (bf16[128,384]{0,1:T(8,128)(2,1)S(1)}, bf16[128,384]{0,1:T(8,128)(2,1)}, u32[]{:S(2)}) copy-start(bf16[128,384]{0,1:T(8,128)(2,1)} %copy-done.20) | copy-start | bytes 294916
  52.3 3.5 %copy-start.13 = (bf16[64,384]{0,1:T(8,128)(2,1)S(1)}, bf16[64,384]{0,1:T(8,128)(2,1)}, u32[]{:S(2)}) copy-start(bf16[64,384]{0,1:T(8,128)(2,1)} %copy-done.12) | copy-start | bytes 147460
  52.3 3.7 %copy-start.15 = (bf16[128,384]{0,1:T(8,128)(2,1)S(1)}, bf16[128,384]{0,1:T(8,128)(2,1)}, u32[]{:S(2)}) copy-start(bf16[128,384]{0,1:T(8,128)(2,1)} %copy-done.14) | copy-start | bytes 294916
  52.6 3.6 %copy-start.9 = (f32[6,64,256]{2,1,0:T(8,128)S(1)}, f32[6,64,256]{2,1,0:T(8,128)}, u32[]{:S(2)}) copy-start(f32[6,64,256]{2,1,0:T(8,128)} %fusion.16) | copy-start | bytes 1179652
  56.5 3.5 %copy-start.32 = (f32[6,64,128]{2,1,0:T(8,128)S(1)}, f32[6,64,128]{2,1,0:T(8,128)}, u32[]{:S(2)}) copy-start(f32[6,64,128]{2,1,0:T(8,128)} %fusion.44) | copy-start | bytes 589828
  58.8 2.2 %copy-start.31 = (f32[6,64,128]{2,1,0:T(8,128)S(1)}, f32[6,64,128]{2,1,0:T(8,128)}, u32[]{:S(2)}) copy-start(f32[6,64,128]{2,1,0:T(8,128)} %fusion.68) | copy-start | bytes 589828
  58.9 99.5 %all-reduce.5.cloned.1.call-start = ((), (), s32[]{:S(2)}) async-start(), calls=%async_computation.1 | async-start | bytes 1179648 | tf_op jit(solution)/shard_map/psum | solution.py:157
  61.7 13.5 %copy-start.39 = (f32[128,384]{1,0:T(8,128)S(1)}, f32[128,384]{1,0:T(8,128)}, u32[]{:S(2)}) copy-start(f32[128,384]{1,0:T(8,128)} %copy.357) | copy-start | bytes 589828
  62.3 54.4 %collective-permute-start.8 = (f32[128,384]{1,0:T(8,128)S(1)}, f32[128,384]{1,0:T(8,128)}, u32[]{:S(2)}, u32[]{:S(2)}) collective-permute-start(f32[128,384]{1,0:T(8,128)S(1)} %copy.351), channel_id=1, source_target_pairs={{0,2},{1,3},{2,0},{3,1},{4,6},{5,7},{6,4},{7,5},{8,10},{9,11},{10,... | collective-permute-start | bytes 589832 | tf_op jit(solution)/shard_map/ppermute | solution.py:10
  64.7 61.2 %collective-permute-start.10 = (f32[128,384]{1,0:T(8,128)S(1)}, f32[128,384]{1,0:T(8,128)}, u32[]{:S(2)}, u32[]{:S(2)}) collective-permute-start(f32[128,384]{1,0:T(8,128)S(1)} %copy.353), channel_id=1, source_target_pairs={{0,1},{1,0},{2,3},{3,2},{4,5},{5,4},{6,7},{7,6},{8,9},{9,8},{10,11... | collective-permute-start | bytes 589832 | tf_op jit(solution)/shard_map/ppermute | solution.py:10
  67.1 59.8 %collective-permute-start.15 = (f32[128,384]{1,0:T(8,128)S(1)}, f32[128,384]{1,0:T(8,128)S(1)}, u32[]{:S(2)}, u32[]{:S(2)}) collective-permute-start(f32[128,384]{1,0:T(8,128)S(1)} %copy.361), channel_id=1, source_target_pairs={{0,1},{1,0},{2,3},{3,2},{4,5},{5,4},{6,7},{7,6},{8,9},{9,8},{10,11... | collective-permute-start | bytes 589832 | tf_op jit(solution)/shard_map/ppermute | solution.py:10
  67.1 8.1 %collective-permute-start.6 = (f32[128,384]{1,0:T(8,128)}, f32[128,384]{1,0:T(8,128)S(1)}, u32[]{:S(2)}, u32[]{:S(2)}) collective-permute-start(f32[128,384]{1,0:T(8,128)} %copy.349), channel_id=1, source_target_pairs={{0,4},{1,5},{2,6},{3,7},{4,0},{5,1},{6,2},{7,3},{8,12},{9,13},{10,... | collective-permute-start | bytes 589832 | tf_op jit(solution)/shard_map/ppermute | solution.py:10
  67.6 53.2 %collective-permute-start.13 = (f32[128,384]{1,0:T(8,128)S(1)}, f32[128,384]{1,0:T(8,128)}, u32[]{:S(2)}, u32[]{:S(2)}) collective-permute-start(f32[128,384]{1,0:T(8,128)S(1)} %copy.359), channel_id=1, source_target_pairs={{0,2},{1,3},{2,0},{3,1},{4,6},{5,7},{6,4},{7,5},{8,10},{9,11},{10,... | collective-permute-start | bytes 589832 | tf_op jit(solution)/shard_map/ppermute | solution.py:10
  75.2 5.6 %collective-permute-start.11 = (f32[128,384]{1,0:T(8,128)S(1)}, f32[128,384]{1,0:T(8,128)S(1)}, u32[]{:S(2)}, u32[]{:S(2)}) collective-permute-start(f32[128,384]{1,0:T(8,128)S(1)} %copy-done.39), channel_id=1, source_target_pairs={{0,4},{1,5},{2,6},{3,7},{4,0},{5,1},{6,2},{7,3},{8,12},{9,13},{10,... | collective-permute-start | bytes 589832 | tf_op jit(solution)/shard_map/ppermute | solution.py:10
  80.8 36.5 %collective-permute-start.7 = (f32[128,384]{1,0:T(8,128)S(1)}, f32[128,384]{1,0:T(8,128)S(1)}, u32[]{:S(2)}, u32[]{:S(2)}) collective-permute-start(f32[128,384]{1,0:T(8,128)S(1)} %select_n.151), channel_id=1, source_target_pairs={{0,2},{1,3},{2,0},{3,1},{4,6},{5,7},{6,4},{7,5},{8,10},{9,11},{10,... | collective-permute-start | bytes 589832 | tf_op jit(solution)/shard_map/ppermute | solution.py:10
  116.8 4.7 %collective-permute-start.12 = (f32[128,384]{1,0:T(8,128)S(1)}, f32[128,384]{1,0:T(8,128)}, u32[]{:S(2)}, u32[]{:S(2)}) collective-permute-start(f32[128,384]{1,0:T(8,128)S(1)} %select_n.159), channel_id=1, source_target_pairs={{0,2},{1,3},{2,0},{3,1},{4,6},{5,7},{6,4},{7,5},{8,10},{9,11},{10,... | collective-permute-start | bytes 589832 | tf_op jit(solution)/shard_map/ppermute | solution.py:10
  118.7 7.2 %collective-permute-start.9 = (f32[128,384]{1,0:T(8,128)S(1)}, f32[128,384]{1,0:T(8,128)S(1)}, u32[]{:S(2)}, u32[]{:S(2)}) collective-permute-start(f32[128,384]{1,0:T(8,128)S(1)} %select_n.155), channel_id=1, source_target_pairs={{0,1},{1,0},{2,3},{3,2},{4,5},{5,4},{6,7},{7,6},{8,9},{9,8},{10,11... | collective-permute-start | bytes 589832 | tf_op jit(solution)/shard_map/ppermute | solution.py:10
  123.0 4.0 %collective-permute-start.14 = (f32[128,384]{1,0:T(8,128)S(1)}, f32[128,384]{1,0:T(8,128)S(1)}, u32[]{:S(2)}, u32[]{:S(2)}) collective-permute-start(f32[128,384]{1,0:T(8,128)S(1)} %select_n.163), channel_id=1, source_target_pairs={{0,1},{1,0},{2,3},{3,2},{4,5},{5,4},{6,7},{7,6},{8,9},{9,8},{10,11... | collective-permute-start | bytes 589832 | tf_op jit(solution)/shard_map/ppermute | solution.py:10
Sparse Core Ops, SparseCore 0:
  59.0 57.7 all-reduce.2
  119.2 39.1 all-reduce.4
